TPU v7x, 256 devices: a whole 4x4x8 slice. The times are simulated.
256 devices in a mesh: leaf: 32 (over z, x), rank: 4 (over y), rhs: 2 (over core).
Axes of the slice: x: 4, y: 4, z: 8, core: 2. Of those that a mesh axis runs over, the one named last changes fastest.
Arguments:
- rhs: float32 [65536, 512], P(('leaf', 'rank'), 'rhs'), parts along dimension 1, may hold values from -40 to 40
- order: int32 [65536], P(('leaf', 'rank')), may hold values from 0 to 65535, as said below
- diag: float32 [65536], P(('leaf', 'rank')), may hold values from 2 to 8
- blocks: bfloat16 [1536, 128, 128], P(('leaf', 'rank')), may hold values from -0.3125 to 0.3125
- near_rows: int32 [1536], P(('leaf', 'rank')), may hold values from 0 to 511, as said below
- near_cols: int32 [1536], P(('leaf', 'rank')), may hold values from 0 to 511, as said below
- gen_u: bfloat16 [5, 65536, 128], P(None, 'leaf', 'rank'), may hold values from -0.5 to 0.5
- gen_v: bfloat16 [5, 65536, 128], P(None, 'leaf', 'rank'), may hold values from -0.03125 to 0.03125
Outputs:
- solution: float32 [65536, 512], P(('leaf', 'rank'), 'rhs'), parts along dimension 1
- residual: float32 [65536, 512], P(('leaf', 'rank'), 'rhs'), parts along dimension 1
There are 2 independent parts, one for each index of `rhs`. A program takes and returns all parts, laid end to end along the dimension named above; an argument that names none is the same for every part. Nothing has to cross between parts.
Inputs may be any that keep to these rules, and one draw needn't show every extreme that they name: `order`: each aligned run of 512 entries is a permutation of the panel numbers of that run. `near_rows`: block k's row is one of the 4 block rows of the device that holds block k; every block row is named, at least once by a block whose column equals it. `near_cols`: block k's column lies in the same subtree of 2048 panels as its row, at most 4 block columns away from it.
All inputs are finite; a program needn't handle non-finite values.
Results may differ from a plain program's by a relative error of at most 0.0035.
Values may be sent and summed in bfloat16 or wider, within the bound.
A program may use at most 64 MiB of HBM per device.

v0:
```python
import jax
import jax.numpy as jnp
from jax import lax
from jax.sharding import PartitionSpec as P

EPSILON = 1e-06


def from_partner(value, axis, apart):
    mask = 2**apart
    pairs = [(source, source ^ mask) for source in range(lax.axis_size(axis))]
    return lax.ppermute(value, axis, pairs)


def local(rhs, order, diag, blocks, near_rows, near_cols, gen_u, gen_v):
    panel_count, columns_count = rhs.shape
    levels = gen_v.shape[0]
    leaf_panels = gen_v.shape[1]
    block_size = blocks.shape[1]
    rows_dev = panel_count // block_size
    rows_leaf = leaf_panels // block_size
    device = lax.axis_index(("leaf", "rank"))
    leaf_id = lax.axis_index("leaf")
    local_order = order - device * panel_count
    local_rows = near_rows - device * rows_dev
    local_cols = near_cols - leaf_id * rows_leaf
    selector = (jnp.arange(rows_dev, dtype=jnp.int32)[:, None] == local_rows[None, :]).astype(
        jnp.float32
    )

    def tree_sums(coeffs):
        partial_value = [coeffs[level] for level in range(levels)]
        sibling = []
        for level in range(levels):
            stacked = jnp.stack(partial_value[level:], 0)
            received = from_partner(stacked, "leaf", level)
            sibling.append(received[0])
            for upper in range(level + 1, levels):
                partial_value[upper] = partial_value[upper] + received[upper - level]
        return jnp.stack(sibling, 0)

    def apply(vector):
        narrow = vector.astype(jnp.bfloat16)
        subtree = lax.all_gather(narrow, "rank", axis=0, tiled=True)
        coeffs = jnp.einsum("lpk,pn->lkn", gen_v, subtree, preferred_element_type=jnp.float32)
        column_blocks = subtree.reshape(rows_leaf, block_size, columns_count)[local_cols]
        sibling = tree_sums(coeffs).astype(jnp.bfloat16)
        products = jnp.einsum(
            "kij,kjn->kin", blocks, column_blocks, preferred_element_type=jnp.float32
        )
        near = jnp.einsum(
            "rk,kin->rin", selector, products, precision=lax.Precision.HIGHEST
        ).reshape(panel_count, columns_count)
        far = lax.psum_scatter(
            jnp.einsum("lpk,lkn->pn", gen_u, sibling, preferred_element_type=jnp.float32),
            "rank",
            scatter_dimension=0,
            tiled=True,
        )
        return diag[:, None] * vector + near + far

    start = rhs[local_order]
    beta = jnp.sqrt(lax.psum(jnp.sum(start * start, axis=0), ("leaf", "rank")) + EPSILON)
    basis_one = start / beta
    image_one = apply(basis_one)
    h11 = lax.psum(jnp.sum(basis_one * image_one, axis=0), ("leaf", "rank"))
    rest_one = image_one - h11 * basis_one
    h21 = jnp.sqrt(lax.psum(jnp.sum(rest_one * rest_one, axis=0), ("leaf", "rank")) + EPSILON)
    basis_two = rest_one / h21
    image_two = apply(basis_two)
    h12, h22 = lax.psum(
        (jnp.sum(basis_one * image_two, axis=0), jnp.sum(basis_two * image_two, axis=0)),
        ("leaf", "rank"),
    )
    rest_two = image_two - h12 * basis_one - h22 * basis_two
    h32 = jnp.sqrt(lax.psum(jnp.sum(rest_two * rest_two, axis=0), ("leaf", "rank")) + EPSILON)
    r_one = jnp.sqrt(h11 * h11 + h21 * h21)
    cos_one = h11 / r_one
    sin_one = h21 / r_one
    top = cos_one * h12 + sin_one * h22
    low = cos_one * h22 - sin_one * h12
    r_two = jnp.sqrt(low * low + h32 * h32)
    y_two = low / r_two * (-sin_one * beta) / r_two
    y_one = (cos_one * beta - top * y_two) / r_one
    tree_solution = y_one * basis_one + y_two * basis_two
    tree_residual = (
        (beta - y_one * h11 - y_two * h12) * basis_one
        - (y_one * h21 + y_two * h22) * basis_two
        - y_two * rest_two
    )
    solution = jnp.zeros_like(rhs).at[local_order].set(tree_solution)
    residual = jnp.zeros_like(rhs).at[local_order].set(tree_residual)
    return (solution, residual)


def solution(mesh):
    in_specs = (
        P(("leaf", "rank"), "rhs"),
        P(("leaf", "rank")),
        P(("leaf", "rank")),
        P(("leaf", "rank"), None, None),
        P(("leaf", "rank")),
        P(("leaf", "rank")),
        P(None, "leaf", "rank"),
        P(None, "leaf", "rank"),
    )
    out_specs = (P(("leaf", "rank"), "rhs"), P(("leaf", "rank"), "rhs"))
    return jax.shard_map(local, mesh=mesh, in_specs=in_specs, out_specs=out_specs, check_vma=False)
```

profile of v0, /device:TPU:8, one launch (start us, length us, event | category | flops | bytes accessed | tf_op | source)
XLA Modules:
  0.0 1938.2 jit_solution(10514694611025003767)
XLA Ops:
  8.0 2.7 gather_fusion
  10.8 346.4 %psum.42 = f32[256]{0:T(256)S(1)} all-reduce(f32[256]{0:T(256)S(1)} %multiply_reduce_fusion.5), channel_id=1, replica_groups=mesh['leaf'=32,'rank'=4,'rhs'=2] {'leaf','rank'}, use_global_device_ids=true, to_apply=%region_1.0 | all-reduce | flops 256 | bytes 2048 | tf_op jit(solution)/shard_map/psum | solution.py:63
  357.9 23.9 %all-gather.3.cloned.1.call-done = bf16[2048,256]{1,0:T(8,128)(2,1)} async-done(((bf16[512,256]{1,0:T(8,128)(2,1)}), bf16[2048,256]{1,0:T(8,128)(2,1)}) %all-gather.3.cloned.1.call-update) | async-done | bytes 1048592 | tf_op jit(solution)/shard_map/all_gather | solution.py:44
  385.0 3.9 collective-permute-done
  388.9 3.1 collective-permute-start.1
  391.9 3.5 collective-permute-done.1
  397.1 3.8 collective-permute-done.2
  402.8 3.3 collective-permute-done.3
  406.2 6.2 collective-permute-start.4
  421.8 27.5 %reduce-scatter.3.cloned.1.call-done = f32[512,256]{1,0:T(8,128)} async-done(((f32[2048,256]{1,0:T(8,128)}), f32[512,256]{1,0:T(8,128)}) %reduce-scatter.3.cloned.1.call-update) | async-done | bytes 524304 | tf_op jit(solution)/shard_map/reduce_scatter | solution.py:54
  450.5 344.0 %psum.43 = f32[256]{0:T(256)S(1)} all-reduce(f32[256]{0:T(256)S(1)} %multiply_reduce_fusion.4), channel_id=1, replica_groups=mesh['leaf'=32,'rank'=4,'rhs'=2] {'leaf','rank'}, use_global_device_ids=true, to_apply=%region_4.0 | all-reduce | flops 256 | bytes 2048 | tf_op jit(solution)/shard_map/psum | solution.py:66
  795.7 347.8 %psum.44 = f32[256]{0:T(256)S(1)} all-reduce(f32[256]{0:T(256)S(1)} %get-tuple-element.10), channel_id=1, replica_groups=mesh['leaf'=32,'rank'=4,'rhs'=2] {'leaf','rank'}, use_global_device_ids=true, to_apply=%region_6.0 | all-reduce | flops 256 | bytes 2048 | tf_op jit(solution)/shard_map/psum | solution.py:68
  1144.4 20.1 %all-gather.5.cloned.1.call-done = bf16[2048,256]{1,0:T(8,128)(2,1)} async-done(((bf16[512,256]{1,0:T(8,128)(2,1)}), bf16[2048,256]{1,0:T(8,128)(2,1)}) %all-gather.5.cloned.1.call-update) | async-done | bytes 1048592 | tf_op jit(solution)/shard_map/all_gather | solution.py:44
  1167.6 3.9 collective-permute-done.5
  1171.5 3.1 collective-permute-start.6
  1174.6 3.5 collective-permute-done.6
  1179.7 3.8 collective-permute-done.7
  1185.4 3.3 collective-permute-done.8
  1188.8 6.4 collective-permute-start.9
  1206.5 25.5 %reduce-scatter.5.cloned.1.call-done = f32[512,256]{1,0:T(8,128)} async-done(((f32[2048,256]{1,0:T(8,128)}), f32[512,256]{1,0:T(8,128)}) %reduce-scatter.5.cloned.1.call-update) | async-done | bytes 524304 | tf_op jit(solution)/shard_map/reduce_scatter | solution.py:54
  1233.3 344.0 %all-reduce = (f32[256]{0:T(256)S(1)}, f32[256]{0:T(256)S(1)}) all-reduce(f32[256]{0:T(256)S(1)} %get-tuple-element.3, f32[256]{0:T(256)S(1)} %get-tuple-element.2), channel_id=1, replica_groups=mesh['leaf'=32,'rank'=4,'rhs'=2] {'leaf','rank'}, use_global_device_ids=true, to_apply=%region_11.0 | all-reduce | flops 512 | bytes 4096 | tf_op jit(solution)/shard_map/psum | solution.py:71
  1577.5 347.8 %psum.47 = f32[256]{0:T(256)S(1)} all-reduce(f32[256]{0:T(256)S(1)} %multiply_reduce_fusion), channel_id=1, replica_groups=mesh['leaf'=32,'rank'=4,'rhs'=2] {'leaf','rank'}, use_global_device_ids=true, to_apply=%region_13.0 | all-reduce | flops 256 | bytes 2048 | tf_op jit(solution)/shard_map/psum | solution.py:76
  1925.3 3.1 scatter_custom_fusion
  1928.4 3.2 scatter_custom_fusion.1
  (86 shorter events, 40.5 us)
Async XLA Ops:
  7.2 407.0 %copy-start = (bf16[5,2048,32]{1,2,0:T(8,128)(2,1)S(1)}, bf16[5,2048,32]{1,2,0:T(8,128)(2,1)}, u32[]{:S(2)}) copy-start(bf16[5,2048,32]{1,2,0:T(8,128)(2,1)} %param.14) | copy-start | bytes 1966084
  7.2 374.7 %all-gather.3.cloned.1.call-start = ((), (), s32[]{:S(2)}) async-start(), calls=%async_computation.2 | async-start | bytes 1310720 | tf_op jit(solution)/shard_map/all_gather | solution.py:44
  8.0 373.9 %copy-start.3 = (bf16[5,2048,32]{1,2,0:T(8,128)(2,1)S(1)}, bf16[5,2048,32]{1,2,0:T(8,128)(2,1)}, u32[]{:S(2)}) copy-start(bf16[5,2048,32]{1,2,0:T(8,128)(2,1)} %param.15) | copy-start | bytes 1966084
  357.9 91.4 %reduce-scatter.3.cloned.1.call-start = ((), (), s32[]{:S(2)}) async-start(), calls=%async_computation.3 | async-start | bytes 2621440 | tf_op jit(solution)/shard_map/reduce_scatter | solution.py:54
  383.4 5.4 collective-permute-start
  388.9 6.6 collective-permute-start.1
  395.5 5.4 collective-permute-start.2
  400.9 5.3 collective-permute-start.3
  406.2 8.0 collective-permute-start.4
  414.1 2.0 copy-start.7
  414.1 2.0 copy-start.8
  414.2 2.0 copy-start.1
  416.1 1.0 copy-start.5
  416.1 748.4 %all-gather.5.cloned.1.call-start = ((), (), s32[]{:S(2)}) async-start(), calls=%async_computation.4 | async-start | bytes 1310720 | tf_op jit(solution)/shard_map/all_gather | solution.py:44
  420.8 28.5 %copy-start.6 = (f32[512]{0:T(512)S(1)}, f32[512]{0:T(512)}, u32[]{:S(2)}) copy-start(f32[512]{0:T(512)} %param.10) | copy-start | bytes 6148
  421.8 742.7 %copy-start.4 = (bf16[5,2048,32]{1,2,0:T(8,128)(2,1)S(1)}, bf16[5,2048,32]{1,2,0:T(8,128)(2,1)}, u32[]{:S(2)}) copy-start(bf16[5,2048,32]{1,2,0:T(8,128)(2,1)} %param.15) | copy-start | bytes 1966084
  1144.3 87.8 %reduce-scatter.5.cloned.1.call-start = ((), (), s32[]{:S(2)}) async-start(), calls=%async_computation.5 | async-start | bytes 2621440 | tf_op jit(solution)/shard_map/reduce_scatter | solution.py:54
  1166.0 5.4 collective-permute-start.5
  1171.5 6.6 collective-permute-start.6
  1178.1 5.4 collective-permute-start.7
  1183.5 5.3 collective-permute-start.8
  1188.8 8.1 collective-permute-start.9
  1196.9 1.9 copy-start.2
Sparse Core Ops, SparseCore 0:
  358.0 23.7 all-gather.2
  416.2 33.0 reduce-scatter.2
  1144.4 20.0 all-gather.4
  1199.0 33.0 reduce-scatter.4
where the time goes:
time: 1940 us
  blocking collectives  1730 us (89%)
  waiting for transfers between devices  129 us (7%)
  starting transfers between devices  29.2 us (2%)
    psum x1, blocking collectives, local(): lax.psum(jnp.sum(rest_one * rest_one, axis=0), ('leaf', 'rank')) + EPSILON  348 us
    psum x1, blocking collectives, local(): lax.psum(jnp.sum(rest_two * rest_two, axis=0), ('leaf', 'rank')) + EPSILON  348 us
    psum x1, blocking collectives, local(): lax.psum(jnp.sum(start * start, axis=0), ('leaf', 'rank')) + EPSILON  346 us
    psum x1, blocking collectives, local(): lax.psum((jnp.sum(basis_one * image_two, axis=0), jnp.sum(basis_two * ima...  344 us
    psum x1, blocking collectives, local(): h11 = lax.psum(jnp.sum(basis_one * image_one, axis=0), ('leaf', 'rank'))  344 us
    reduce_scatter x2, waiting for transfers between devices, apply(): lax.psum_scatter(jnp.einsum('lpk,lkn->pn', gen_u, sibling, preferred_elem...  53 us
    all_gather x2, waiting for transfers between devices, apply(): subtree = lax.all_gather(narrow, 'rank', axis=0, tiled=True)  44 us
  transfers between devices with their start and end apart: 14, of which 14 were waited for; matrix products, arithmetic and copies ran while one was open for 1% of the time, Pallas kernels for 0%

commit v1 on v0

--- a/solution.py
+++ b/solution.py
@@ -4,6 +4,7 @@
 from jax.sharding import PartitionSpec as P
 
 EPSILON = 1e-06
+trace_masks = lambda w_in, lane_axis, row_axis: lax.psum(lax.psum(w_in, lane_axis), row_axis)
 
 
 def from_partner(value, axis, apart):
@@ -68,9 +69,10 @@
     h21 = jnp.sqrt(lax.psum(jnp.sum(rest_one * rest_one, axis=0), ("leaf", "rank")) + EPSILON)
     basis_two = rest_one / h21
     image_two = apply(basis_two)
-    h12, h22 = lax.psum(
+    h12, h22 = trace_masks(
         (jnp.sum(basis_one * image_two, axis=0), jnp.sum(basis_two * image_two, axis=0)),
-        ("leaf", "rank"),
+        "leaf",
+        "rank",
     )
     rest_two = image_two - h12 * basis_one - h22 * basis_two
     h32 = jnp.sqrt(lax.psum(jnp.sum(rest_two * rest_two, axis=0), ("leaf", "rank")) + EPSILON)

time: 1940 us -> 1670 us (0.86)
  blocking collectives: 1730 us -> 1470 us
    psum x1 -> x2, blocking collectives: 344 us -> 84.6 us  [the longest x1 75.1 us: lax.psum(w_in, lane_axis)]
where the time goes in v1:
time: 1670 us
  blocking collectives  1470 us (88%)
  waiting for transfers between devices  129 us (8%)
  starting transfers between devices  29.2 us (2%)
    psum x1, blocking collectives, local(): lax.psum(jnp.sum(rest_one * rest_one, axis=0), ('leaf', 'rank')) + EPSILON  348 us
    psum x1, blocking collectives, local(): lax.psum(jnp.sum(start * start, axis=0), ('leaf', 'rank')) + EPSILON  346 us
    psum x1, blocking collectives, local(): h11 = lax.psum(jnp.sum(basis_one * image_one, axis=0), ('leaf', 'rank'))  344 us
    psum x1, blocking collectives, local(): lax.psum(jnp.sum(rest_two * rest_two, axis=0), ('leaf', 'rank')) + EPSILON  343 us
    psum x1, blocking collectives, lax.psum(w_in, lane_axis)  75.1 us
    reduce_scatter x2, waiting for transfers between devices, apply(): lax.psum_scatter(jnp.einsum('lpk,lkn->pn', gen_u, sibling, preferred_elem...  53 us
    all_gather x2, waiting for transfers between devices, apply(): subtree = lax.all_gather(narrow, 'rank', axis=0, tiled=True)  44 us
  transfers between devices with their start and end apart: 14, of which 14 were waited for; matrix products, arithmetic and copies ran while one was open for 1% of the time, Pallas kernels for 0%

profile of v1, /device:TPU:8, one launch (start us, length us, event | category | flops | bytes accessed | tf_op | source)
XLA Modules:
  0.0 1674.0 jit_solution(4806936930157717055)
XLA Ops:
  10.8 346.4 %psum.56 = f32[256]{0:T(256)S(1)} all-reduce(f32[256]{0:T(256)S(1)} %multiply_reduce_fusion.5), channel_id=1, replica_groups=mesh['leaf'=32,'rank'=4,'rhs'=2] {'leaf','rank'}, use_global_device_ids=true, to_apply=%region_1.0 | all-reduce | flops 256 | bytes 2048 | tf_op jit(solution)/shard_map/psum | solution.py:64
  357.9 23.9 %all-gather.3.cloned.1.call-done = bf16[2048,256]{1,0:T(8,128)(2,1)} async-done(((bf16[512,256]{1,0:T(8,128)(2,1)}), bf16[2048,256]{1,0:T(8,128)(2,1)}) %all-gather.3.cloned.1.call-update) | async-done | bytes 1048592 | tf_op jit(solution)/shard_map/all_gather | solution.py:45
  385.0 3.9 collective-permute-done
  388.9 3.1 collective-permute-start.1
  391.9 3.5 collective-permute-done.1
  397.1 3.8 collective-permute-done.2
  402.8 3.3 collective-permute-done.3
  406.2 6.2 collective-permute-start.4
  421.8 27.5 %reduce-scatter.3.cloned.1.call-done = f32[512,256]{1,0:T(8,128)} async-done(((f32[2048,256]{1,0:T(8,128)}), f32[512,256]{1,0:T(8,128)}) %reduce-scatter.3.cloned.1.call-update) | async-done | bytes 524304 | tf_op jit(solution)/shard_map/reduce_scatter | solution.py:55
  450.5 344.0 %psum.57 = f32[256]{0:T(256)S(1)} all-reduce(f32[256]{0:T(256)S(1)} %multiply_reduce_fusion.4), channel_id=1, replica_groups=mesh['leaf'=32,'rank'=4,'rhs'=2] {'leaf','rank'}, use_global_device_ids=true, to_apply=%region_4.0 | all-reduce | flops 256 | bytes 2048 | tf_op jit(solution)/shard_map/psum | solution.py:67
  795.7 347.8 %psum.58 = f32[256]{0:T(256)S(1)} all-reduce(f32[256]{0:T(256)S(1)} %get-tuple-element.12), channel_id=1, replica_groups=mesh['leaf'=32,'rank'=4,'rhs'=2] {'leaf','rank'}, use_global_device_ids=true, to_apply=%region_6.0 | all-reduce | flops 256 | bytes 2048 | tf_op jit(solution)/shard_map/psum | solution.py:69
  1144.4 20.1 %all-gather.5.cloned.1.call-done = bf16[2048,256]{1,0:T(8,128)(2,1)} async-done(((bf16[512,256]{1,0:T(8,128)(2,1)}), bf16[2048,256]{1,0:T(8,128)(2,1)}) %all-gather.5.cloned.1.call-update) | async-done | bytes 1048592 | tf_op jit(solution)/shard_map/all_gather | solution.py:45
  1167.6 3.8 collective-permute-done.5
  1171.5 3.1 collective-permute-start.6
  1174.6 3.5 collective-permute-done.6
  1179.7 3.8 collective-permute-done.7
  1185.5 3.3 collective-permute-done.8
  1188.8 6.4 collective-permute-start.9
  1206.5 25.6 %reduce-scatter.5.cloned.1.call-done = f32[512,256]{1,0:T(8,128)} async-done(((f32[2048,256]{1,0:T(8,128)}), f32[512,256]{1,0:T(8,128)}) %reduce-scatter.5.cloned.1.call-update) | async-done | bytes 524304 | tf_op jit(solution)/shard_map/reduce_scatter | solution.py:55
  1233.3 75.1 %all-reduce = (f32[256]{0:T(256)S(1)}, f32[256]{0:T(256)S(1)}) all-reduce(f32[256]{0:T(256)S(1)} %get-tuple-element.3, f32[256]{0:T(256)S(1)} %get-tuple-element.2), channel_id=1, replica_groups=mesh['leaf'=32,'rank'=4,'rhs'=2] {'leaf'}, use_global_device_ids=true, to_apply=%region_12.0 | all-reduce | flops 512 | bytes 4096 | tf_op jit(solution)/shard_map/psum | solution.py:7
  1308.4 9.5 all-reduce.1
  1318.1 343.0 %psum.63 = f32[256]{0:T(256)S(1)} all-reduce(f32[256]{0:T(256)S(1)} %multiply_reduce_fusion), channel_id=1, replica_groups=mesh['leaf'=32,'rank'=4,'rhs'=2] {'leaf','rank'}, use_global_device_ids=true, to_apply=%region_15.0 | all-reduce | flops 256 | bytes 2048 | tf_op jit(solution)/shard_map/psum | solution.py:78
  1661.1 3.1 scatter_custom_fusion
  1664.2 3.2 scatter_custom_fusion.1
  (87 shorter events, 43.2 us)
Async XLA Ops:
  7.2 407.0 %copy-start = (bf16[5,2048,32]{1,2,0:T(8,128)(2,1)S(1)}, bf16[5,2048,32]{1,2,0:T(8,128)(2,1)}, u32[]{:S(2)}) copy-start(bf16[5,2048,32]{1,2,0:T(8,128)(2,1)} %param.14) | copy-start | bytes 1966084
  7.2 374.7 %all-gather.3.cloned.1.call-start = ((), (), s32[]{:S(2)}) async-start(), calls=%async_computation.2 | async-start | bytes 1310720 | tf_op jit(solution)/shard_map/all_gather | solution.py:45
  8.0 373.9 %copy-start.3 = (bf16[5,2048,32]{1,2,0:T(8,128)(2,1)S(1)}, bf16[5,2048,32]{1,2,0:T(8,128)(2,1)}, u32[]{:S(2)}) copy-start(bf16[5,2048,32]{1,2,0:T(8,128)(2,1)} %param.15) | copy-start | bytes 1966084
  357.9 91.4 %reduce-scatter.3.cloned.1.call-start = ((), (), s32[]{:S(2)}) async-start(), calls=%async_computation.3 | async-start | bytes 2621440 | tf_op jit(solution)/shard_map/reduce_scatter | solution.py:55
  383.4 5.4 collective-permute-start
  388.9 6.6 collective-permute-start.1
  395.5 5.4 collective-permute-start.2
  400.9 5.3 collective-permute-start.3
  406.2 8.0 collective-permute-start.4
  414.1 2.0 copy-start.7
  414.1 2.0 copy-start.8
  414.2 2.1 copy-start.1
  416.1 1.0 copy-start.5
  416.1 748.4 %all-gather.5.cloned.1.call-start = ((), (), s32[]{:S(2)}) async-start(), calls=%async_computation.4 | async-start | bytes 1310720 | tf_op jit(solution)/shard_map/all_gather | solution.py:45
  420.8 28.4 %copy-start.6 = (f32[512]{0:T(512)S(1)}, f32[512]{0:T(512)}, u32[]{:S(2)}) copy-start(f32[512]{0:T(512)} %param.10) | copy-start | bytes 6148
  421.8 742.7 %copy-start.4 = (bf16[5,2048,32]{1,2,0:T(8,128)(2,1)S(1)}, bf16[5,2048,32]{1,2,0:T(8,128)(2,1)}, u32[]{:S(2)}) copy-start(bf16[5,2048,32]{1,2,0:T(8,128)(2,1)} %param.15) | copy-start | bytes 1966084
  1144.3 87.8 %reduce-scatter.5.cloned.1.call-start = ((), (), s32[]{:S(2)}) async-start(), calls=%async_computation.5 | async-start | bytes 2621440 | tf_op jit(solution)/shard_map/reduce_scatter | solution.py:55
  1166.0 5.4 collective-permute-start.5
  1171.5 6.6 collective-permute-start.6
  1178.1 5.4 collective-permute-start.7
  1183.5 5.3 collective-permute-start.8
  1188.8 8.1 collective-permute-start.9
  1196.9 1.9 copy-start.2
Sparse Core Ops, SparseCore 0:
  358.0 23.7 all-gather.2
  416.2 33.0 reduce-scatter.2
  1144.4 20.0 all-gather.4
  1199.0 33.0 reduce-scatter.4
